TPU v7x, 512 devices: a whole 4x8x8 slice. The times are simulated.
512 devices in a mesh: ctx: 64 (over z, y_hi, core), exp: 8 (over x, y_lo).
Axes of the slice: x: 4, y: 8 (y_hi: 4, y_lo: 2; y = y_hi * 2 + y_lo), z: 8, core: 2. Of those that a mesh axis runs over, the one named last changes fastest.
Arguments:
- residual: bfloat16 [4096, 2048], P('ctx', 'exp'), may hold values from -60 to 60
- queries: bfloat16 [4096, 2048], P('ctx', 'exp'), may hold values from -6.5 to 6.5
- keys: bfloat16 [4096, 2048], P('ctx', 'exp'), may hold values from -6.5 to 6.5
- values: bfloat16 [4096, 2048], P('ctx', 'exp'), may hold values from -6 to 6
- out_proj: bfloat16 [2048, 2048], P(None, 'exp'), may hold values from -0.5 to 0.5
- norm_gain: float32 [2048], replicated, may hold values from 0.1 to 1.9
- w_gate: bfloat16 [8, 2048, 8192], P('exp', None, 'ctx'), may hold values from -0.125 to 0.125
- w_up: bfloat16 [8, 2048, 8192], P('exp', None, 'ctx'), may hold values from -0.125 to 0.125
- w_down: bfloat16 [8, 8192, 2048], P('exp', 'ctx'), may hold values from -0.0625 to 0.0625
- routes: int32 [4096, 1], P('ctx'), may hold values from 0 to 7; in each aligned block of 64 rows (0 to 63, 64 to 127, ...) at most 8 rows name the same one
- block_mask: int32 [32, 32], replicated, may hold values from 0 to 1, as said below
Outputs:
- mixed: bfloat16 [8, 512, 2048], P('exp', 'ctx')
Inputs may be any that keep to these rules, and one draw needn't show every extreme that they name: `routes`: each stored row is named by exactly 8 of the 64 rows of one index of ctx. `block_mask`: every diagonal entry is 1.
All inputs are finite; a program needn't handle non-finite values.
Results may differ from a plain program's by a relative error of at most 0.006.
Values may be sent and summed in bfloat16 or wider, within the bound.
A program may use at most 64 MiB of HBM per device.

v0:
```python
import math
import jax
import jax.numpy as jnp
from jax import lax
from jax.sharding import PartitionSpec as P

HD = 128
BLK = 128


def body(
    residual, queries, keys, values, out_proj, norm_gain, w_gate, w_up, w_down, routes, block_mask
):
    local_tokens = residual.shape[0]
    local_width = queries.shape[1]
    heads_here = local_width // HD
    blocks_all = block_mask.shape[0]
    expert_count = lax.axis_size("exp")
    per_expert = local_tokens // expert_count
    scaling = 1.0 / math.sqrt(HD)
    ctx_place = lax.axis_index("ctx")
    query_pos = ctx_place * local_tokens + jnp.arange(local_tokens, dtype=jnp.int32)
    query_blocks = jax.nn.one_hot(query_pos // BLK, blocks_all, dtype=jnp.float32)
    query_mask = jnp.dot(query_blocks, block_mask.astype(jnp.float32))
    query_three = queries.reshape(local_tokens, heads_here, HD)
    key_piece = lax.all_gather(keys, "ctx", axis=0, tiled=True)
    value_piece = lax.all_gather(values, "ctx", axis=0, tiled=True)
    count_here = key_piece.shape[0]
    key_pos = jnp.arange(count_here, dtype=jnp.int32)
    key_blocks = jax.nn.one_hot(key_pos // BLK, blocks_all, dtype=jnp.float32)
    allowed = jnp.dot(query_mask, key_blocks.T) > 0.5
    top_old = jnp.full((heads_here, local_tokens), -1e30, jnp.float32)
    key_three = key_piece.reshape(count_here, heads_here, HD)
    value_three = value_piece.reshape(count_here, heads_here, HD)
    scores = (
        jnp.einsum("qhd,khd->hqk", query_three, key_three, preferred_element_type=jnp.float32)
        * scaling
    )
    scores = jnp.where(allowed[None], scores, -1e30)
    top_new = jnp.maximum(top_old, jnp.max(scores, axis=2))
    exponent = jnp.where(allowed[None], jnp.exp(scores - top_new[:, :, None]), 0.0)
    total_new = jnp.sum(exponent, axis=2)
    product = jnp.einsum(
        "hqk,khd->hqd",
        exponent.astype(jnp.bfloat16),
        value_three,
        preferred_element_type=jnp.float32,
    )
    attended = (product / total_new[:, :, None]).astype(jnp.bfloat16)
    attended = attended.transpose(1, 0, 2).reshape(local_tokens, local_width)
    projected = jnp.dot(
        lax.all_gather(attended, "exp", axis=1, tiled=True),
        out_proj,
        preferred_element_type=jnp.float32,
    )
    hidden = (residual.astype(jnp.float32) + projected).astype(jnp.bfloat16)
    target = routes[:, 0]
    token_ids = jnp.arange(local_tokens, dtype=jnp.int32)
    earlier = (target[:, None] == target[None, :]) & (token_ids[None, :] < token_ids[:, None])
    ranking = jnp.sum(earlier.astype(jnp.int32), axis=1)
    slot_of = target * per_expert + ranking
    slot_ids = jnp.arange(expert_count * per_expert, dtype=jnp.int32)
    placing = (slot_of[None, :] == slot_ids[:, None]).astype(jnp.bfloat16)
    send_buffer = jnp.dot(placing, hidden, preferred_element_type=jnp.float32).astype(jnp.bfloat16)
    send_buffer = send_buffer.reshape(expert_count, per_expert, hidden.shape[1])
    own_rows = lax.all_to_all(send_buffer, "exp", split_axis=0, concat_axis=2, tiled=True)[0]
    values_f = own_rows.astype(jnp.float32)
    meansq = jnp.mean(values_f * values_f, axis=1, keepdims=True)
    normed_own = (values_f * lax.rsqrt(meansq + 1e-05) * norm_gain).astype(jnp.bfloat16)
    normed_rows = lax.all_gather(normed_own, "ctx", axis=0, tiled=True)
    gate_v = jnp.dot(normed_rows, w_gate[0], preferred_element_type=jnp.float32)
    up_v = jnp.dot(normed_rows, w_up[0], preferred_element_type=jnp.float32)
    activ = (jax.nn.silu(gate_v) * up_v).astype(jnp.bfloat16)
    terms = jnp.dot(activ, w_down[0], preferred_element_type=jnp.float32)
    summed = lax.psum_scatter(terms, "ctx", scatter_dimension=0, tiled=True)
    return (own_rows.astype(jnp.float32) + summed).astype(jnp.bfloat16)[None]


def solution(mesh):
    in_specs = (
        P("ctx", "exp"),
        P("ctx", "exp"),
        P("ctx", "exp"),
        P("ctx", "exp"),
        P(None, "exp"),
        P(),
        P("exp", None, "ctx"),
        P("exp", None, "ctx"),
        P("exp", "ctx", None),
        P("ctx", None),
        P(),
    )
    out_specs = P("exp", "ctx", None)
    return jax.shard_map(body, mesh=mesh, in_specs=in_specs, out_specs=out_specs, check_vma=False)
```

profile of v0, /device:TPU:2, one launch (start us, length us, event | category | flops | bytes accessed | tf_op | source)
XLA Modules:
  0.0 478.8 jit_solution(12788094995489610600)
XLA Ops:
  6.5 0.0 copy-start
  6.5 0.0 all-gather.4.cloned.1.call-start
  6.5 0.7 all-gather.4.cloned.1.call-update
  7.3 0.0 all-gather.6.cloned.1.call-start
  7.3 0.7 all-gather.6.cloned.1.call-update
  8.0 0.0 all-gather.8.cloned.1.call-start
  8.1 0.9 convert_reduce_fusion
  9.0 0.7 multiply_add_fusion
  9.7 1.3 convolution_compare_fusion
  10.9 0.0 copy-start.3
  10.9 89.1 %all-gather.4.cloned.1.call-done = bf16[4096,256]{1,0:T(8,128)(2,1)} async-done(((bf16[64,256]{1,0:T(8,128)(2,1)}), bf16[4096,256]{1,0:T(8,128)(2,1)}) %all-gather.4.cloned.1.call-update) | async-done | bytes 2097168 | tf_op jit(solution)/shard_map/all_gather | solution.py:26
  100.0 4.1 copy.25
  104.1 2.4 fusion.43
  106.5 0.7 fusion.1
  107.1 76.6 %all-gather.6.cloned.1.call-done = bf16[4096,256]{1,0:T(8,128)(2,1)} async-done(((bf16[64,256]{1,0:T(8,128)(2,1)}), bf16[4096,256]{1,0:T(8,128)(2,1)}) %all-gather.6.cloned.1.call-update) | async-done | bytes 2097168 | tf_op jit(solution)/shard_map/all_gather | solution.py:27
  183.7 4.1 copy.28
  187.8 2.5 fusion.8
  190.3 26.8 %all_gather.14 = bf16[64,2048]{1,0:T(8,128)(2,1)S(1)} all-gather(bf16[64,256]{1,0:T(8,128)(2,1)S(1)} %bitcast.56), channel_id=1, replica_groups=mesh['ctx'=64,'exp'=8] {'exp'}, dimensions={1}, use_global_device_ids=true | all-gather | bytes 294912 | tf_op jit(solution)/shard_map/all_gather | solution.py:52
  217.1 0.0 copy-done
  217.1 0.4 fusion.9
  217.5 11.1 %all_to_all.4 = bf16[8,8,256]{2,1,0:T(8,128)(2,1)S(1)} all-to-all(bf16[8,8,256]{2,1,0:T(8,128)(2,1)S(1)} %fusion.9), channel_id=1, replica_groups=mesh['ctx'=64,'exp'=8] {'exp'}, dimensions={0} | all-to-all | bytes 65536 | tf_op jit(solution)/shard_map/all_to_all | solution.py:66
  228.6 0.1 multiply_reduce_fusion
  228.8 0.7 multiply_convert_fusion
  229.5 0.0 all-gather.8.cloned.1.call-update
  229.5 0.0 reduce-scatter.2.cloned.1.call-start
  229.6 80.5 %all-gather.8.cloned.1.call-done = bf16[512,2048]{1,0:T(8,128)(2,1)} async-done(((bf16[8,2048]{1,0:T(8,128)(2,1)}), bf16[512,2048]{1,0:T(8,128)(2,1)}) %all-gather.8.cloned.1.call-update) | async-done | bytes 2097168 | tf_op jit(solution)/shard_map/all_gather | solution.py:70
  310.0 2.5 fusion.19
  312.6 0.0 copy-done.1
  312.6 5.4 %fusion.4 = f32[512,2048]{1,0:T(8,128)} fusion(bf16[512,2048]{1,0:T(8,128)(2,1)S(1)} %copy-done.1, bf16[1,128,2048]{2,1,0:T(8,128)(2,1)} %param.19, bf16[1,2048,128]{2,1,0:T(8,128)(2,1)} %param.18, f32[512,128]{1,0:T(8,128)S(1)} %fusion.19), kind=kOutput, calls=%fused_computation.8 | convolution fusion | flops 537264128 | bytes 7602176 | tf_op jit(solution)/shard_map/dot_general | solution.py:74
  318.0 0.0 reduce-scatter.2.cloned.1.call-update
  318.0 152.8 %reduce-scatter.2.cloned.1.call-done = f32[8,2048]{1,0:T(8,128)} async-done(((f32[512,2048]{1,0:T(8,128)}), f32[8,2048]{1,0:T(8,128)}) %reduce-scatter.2.cloned.1.call-update) | async-done | bytes 65552 | tf_op jit(solution)/shard_map/reduce_scatter | solution.py:75
  470.8 1.5 fusion.29
  (12 shorter events, 0.1 us)
Async XLA Ops:
  6.5 210.6 %copy-start = (bf16[2048,256]{1,0:T(8,128)(2,1)S(1)}, bf16[2048,256]{1,0:T(8,128)(2,1)}, u32[]{:S(2)}) copy-start(bf16[2048,256]{1,0:T(8,128)(2,1)} %param.15) | copy-start | bytes 3145732
  6.5 93.5 %all-gather.4.cloned.1.call-start = ((), (), s32[]{:S(2)}) async-start(), calls=%async_computation.2 | async-start | bytes 2129920 | tf_op jit(solution)/shard_map/all_gather | solution.py:26
  7.3 176.5 %all-gather.6.cloned.1.call-start = ((), (), s32[]{:S(2)}) async-start(), calls=%async_computation.3 | async-start | bytes 2129920 | tf_op jit(solution)/shard_map/all_gather | solution.py:27
  8.0 302.0 %all-gather.8.cloned.1.call-start = ((), (), s32[]{:S(2)}) async-start(), calls=%async_computation.4 | async-start | bytes 2129920 | tf_op jit(solution)/shard_map/all_gather | solution.py:70
  10.9 93.2 %copy-start.3 = (bf16[64,256]{1,0:T(8,128)(2,1)S(1)}, bf16[64,256]{1,0:T(8,128)(2,1)}, u32[]{:S(2)}) copy-start(bf16[64,256]{1,0:T(8,128)(2,1)} %param.12) | copy-start | bytes 98308
  187.8 29.3 %copy-start.2 = (bf16[64,256]{1,0:T(8,128)(2,1)S(1)}, bf16[64,256]{1,0:T(8,128)(2,1)}, u32[]{:S(2)}) copy-start(bf16[64,256]{1,0:T(8,128)(2,1)} %param.11) | copy-start | bytes 98308
  187.8 40.9 %copy-start.4 = (f32[2048]{0:T(1024)S(1)}, f32[2048]{0:T(1024)}, u32[]{:S(2)}) copy-start(f32[2048]{0:T(1024)} %param.16) | copy-start | bytes 24580
  229.5 241.3 %reduce-scatter.2.cloned.1.call-start = ((), (), s32[]{:S(2)}) async-start(), calls=%async_computation.5 | async-start | bytes 4259840 | tf_op jit(solution)/shard_map/reduce_scatter | solution.py:75
  310.0 2.5 copy-start.1
Sparse Core Ops, SparseCore 0:
  10.7 89.2 all-gather.3
  103.3 80.3 all-gather.5
  229.6 80.3 all-gather.7
  318.2 152.6 reduce-scatter.1
where the time goes:
time: 479 us
  waiting for transfers between devices  400 us (84%)
  blocking collectives  37.9 us (8%)
  matrix products  14.5 us (3%)
  between operations  13.2 us (3%)
  local copies, waits for them, and re-layouts  8.24 us (2%)
    reduce_scatter x1, waiting for transfers between devices, body(): summed = lax.psum_scatter(terms, 'ctx', scatter_dimension=0, tiled=True)  153 us
    all_gather x1, waiting for transfers between devices, body(): key_piece = lax.all_gather(keys, 'ctx', axis=0, tiled=True)  89.1 us
    all_gather x1, waiting for transfers between devices, body(): normed_rows = lax.all_gather(normed_own, 'ctx', axis=0, tiled=True)  80.5 us
    all_gather x1, waiting for transfers between devices, body(): value_piece = lax.all_gather(values, 'ctx', axis=0, tiled=True)  76.6 us
    all_gather x1, blocking collectives, body(): lax.all_gather(attended, 'exp', axis=1, tiled=True)  26.8 us
    all_to_all x1, blocking collectives, body(): lax.all_to_all(send_buffer, 'exp', split_axis=0, concat_axis=2, tiled=True)  11.1 us
  transfers between devices with their start and end apart: 4, of which 4 were waited for; matrix products, arithmetic and copies ran while one was open for 2% of the time, Pallas kernels for 0%

commit v1 on v0

--- a/solution.py
+++ b/solution.py
@@ -23,7 +23,9 @@
     query_blocks = jax.nn.one_hot(query_pos // BLK, blocks_all, dtype=jnp.float32)
     query_mask = jnp.dot(query_blocks, block_mask.astype(jnp.float32))
     query_three = queries.reshape(local_tokens, heads_here, HD)
-    key_piece = lax.all_gather(keys, "ctx", axis=0, tiled=True)
+    key_piece = jnp.concatenate(
+        lax.all_to_all(jnp.stack([keys] * lax.axis_size("ctx")), "ctx", 0, 0), axis=0
+    )
     value_piece = lax.all_gather(values, "ctx", axis=0, tiled=True)
     count_here = key_piece.shape[0]
     key_pos = jnp.arange(count_here, dtype=jnp.int32)

time: 479 us -> 428 us (0.89)
  the two profiles are of different devices: /device:TPU:2 before, /device:TPU:4 now
where the time goes in v1:
time: 428 us
  waiting for transfers between devices  335 us (78%)
  blocking collectives  37 us (9%)
  starting transfers between devices  16.8 us (4%)
  matrix products  14 us (3%)
  between operations  13.2 us (3%)
  local copies, waits for them, and re-layouts  8.6 us (2%)
    reduce_scatter x1, waiting for transfers between devices, body(): summed = lax.psum_scatter(terms, 'ctx', scatter_dimension=0, tiled=True)  153 us
    all_gather x1, waiting for transfers between devices, body(): normed_rows = lax.all_gather(normed_own, 'ctx', axis=0, tiled=True)  81.3 us
    all_to_all x1, waiting for transfers between devices, body(): lax.all_to_all(jnp.stack([keys] * lax.axis_size('ctx')), 'ctx', 0, 0)  65.5 us
    all_gather x1, waiting for transfers between devices, body(): value_piece = lax.all_gather(values, 'ctx', axis=0, tiled=True)  34.8 us
    all_gather x1, blocking collectives, body(): lax.all_gather(attended, 'exp', axis=1, tiled=True)  25.4 us
    all_to_all x1, starting transfers between devices, body(): lax.all_to_all(jnp.stack([keys] * lax.axis_size('ctx')), 'ctx', 0, 0)  16.7 us
    all_to_all x1, blocking collectives, body(): lax.all_to_all(send_buffer, 'exp', split_axis=0, concat_axis=2, tiled=True)  11.6 us
  transfers between devices with their start and end apart: 4, of which 4 were waited for; matrix products, arithmetic and copies ran while one was open for 1% of the time, Pallas kernels for 0%

profile of v1, /device:TPU:4, one launch (start us, length us, event | category | flops | bytes accessed | tf_op | source)
XLA Modules:
  0.0 428.0 jit_solution(17210845377181707493)
XLA Ops:
  6.5 2.4 stack.2
  8.9 16.7 %all-to-all-start = ((bf16[64,64,256]{2,1,0:T(8,128)(2,1)}), bf16[64,64,256]{2,1,0:T(8,128)(2,1)S(1)}, u32[]{:S(2)}, u32[]{:S(2)}) async-start(bf16[64,64,256]{2,1,0:T(8,128)(2,1)} %stack.2), calls=%async_computation | async-start | bytes 4194304 | tf_op jit(solution)/shard_map/all_to_all | solution.py:27
  25.7 0.0 all-gather.3.cloned.1.call-start
  25.7 0.7 all-gather.3.cloned.1.call-update
  26.4 0.0 all-gather.5.cloned.1.call-start
  26.5 0.2 convert_reduce_fusion
  26.7 0.5 convolution_compare_fusion
  27.2 0.0 copy-start.4
  27.3 65.5 %all-to-all-done = bf16[64,64,256]{2,1,0:T(8,128)(2,1)S(1)} async-done(((bf16[64,64,256]{2,1,0:T(8,128)(2,1)}), bf16[64,64,256]{2,1,0:T(8,128)(2,1)S(1)}, u32[]{:S(2)}, u32[]{:S(2)}) %all-to-all-start) | async-done | bytes 2097184 | tf_op jit(solution)/shard_map/all_to_all | solution.py:27
  92.8 2.0 reshape_reshape.3
  94.8 0.0 copy-done.4
  94.8 2.6 fusion.44
  97.4 0.7 fusion.2
  98.1 34.8 %all-gather.3.cloned.1.call-done = bf16[4096,256]{1,0:T(8,128)(2,1)} async-done(((bf16[64,256]{1,0:T(8,128)(2,1)}), bf16[4096,256]{1,0:T(8,128)(2,1)}) %all-gather.3.cloned.1.call-update) | async-done | bytes 2097168 | tf_op jit(solution)/shard_map/all_gather | solution.py:29
  132.9 4.1 copy.25
  137.0 2.5 fusion.9
  139.6 25.4 %all_gather.10 = bf16[64,2048]{1,0:T(8,128)(2,1)S(1)} all-gather(bf16[64,256]{1,0:T(8,128)(2,1)S(1)} %bitcast.53), channel_id=1, replica_groups=mesh['ctx'=64,'exp'=8] {'exp'}, dimensions={1}, use_global_device_ids=true | all-gather | bytes 294912 | tf_op jit(solution)/shard_map/all_gather | solution.py:54
  164.9 0.0 copy-done
  164.9 0.4 fusion.10
  165.4 11.6 %all_to_all.14 = bf16[8,8,256]{2,1,0:T(8,128)(2,1)S(1)} all-to-all(bf16[8,8,256]{2,1,0:T(8,128)(2,1)S(1)} %fusion.10), channel_id=1, replica_groups=mesh['ctx'=64,'exp'=8] {'exp'}, dimensions={0} | all-to-all | bytes 65536 | tf_op jit(solution)/shard_map/all_to_all | solution.py:68
  177.0 0.1 multiply_reduce_fusion
  177.1 0.0 copy-done.3
  177.1 0.7 multiply_convert_fusion
  177.8 0.0 all-gather.5.cloned.1.call-update
  177.9 0.0 reduce-scatter.2.cloned.1.call-start
  177.9 81.3 %all-gather.5.cloned.1.call-done = bf16[512,2048]{1,0:T(8,128)(2,1)} async-done(((bf16[8,2048]{1,0:T(8,128)(2,1)}), bf16[512,2048]{1,0:T(8,128)(2,1)}) %all-gather.5.cloned.1.call-update) | async-done | bytes 2097168 | tf_op jit(solution)/shard_map/all_gather | solution.py:72
  259.2 2.5 fusion.20
  261.8 0.0 copy-done.1
  261.8 5.4 %fusion.5 = f32[512,2048]{1,0:T(8,128)} fusion(bf16[512,2048]{1,0:T(8,128)(2,1)S(1)} %copy-done.1, bf16[1,128,2048]{2,1,0:T(8,128)(2,1)} %param.19, bf16[1,2048,128]{2,1,0:T(8,128)(2,1)} %param.18, f32[512,128]{1,0:T(8,128)S(1)} %fusion.20), kind=kOutput, calls=%fused_computation.9 | convolution fusion | flops 537264128 | bytes 7602176 | tf_op jit(solution)/shard_map/dot_general | solution.py:76
  267.2 0.0 reduce-scatter.2.cloned.1.call-update
  267.2 152.8 %reduce-scatter.2.cloned.1.call-done = f32[8,2048]{1,0:T(8,128)} async-done(((f32[512,2048]{1,0:T(8,128)}), f32[8,2048]{1,0:T(8,128)}) %reduce-scatter.2.cloned.1.call-update) | async-done | bytes 65552 | tf_op jit(solution)/shard_map/reduce_scatter | solution.py:77
  420.0 1.5 fusion.30
  (16 shorter events, 0.1 us)
Async XLA Ops:
  6.5 158.4 %copy-start = (bf16[2048,256]{1,0:T(8,128)(2,1)S(1)}, bf16[2048,256]{1,0:T(8,128)(2,1)}, u32[]{:S(2)}) copy-start(bf16[2048,256]{1,0:T(8,128)(2,1)} %param.15) | copy-start | bytes 3145732
  8.9 17.5 %copy-start.6 = (s32[64,1]{0,1:T(1,128)S(1)}, s32[64,1]{0,1:T(1,128)}, u32[]{:S(2)}) copy-start(s32[64,1]{0,1:T(1,128)} %param.20) | copy-start | bytes 772
  8.9 17.7 %copy-start.5 = (s32[32,32]{1,0:T(8,128)S(1)}, s32[32,32]{1,0:T(8,128)}, u32[]{:S(2)}) copy-start(s32[32,32]{1,0:T(8,128)} %param.21) | copy-start | bytes 12292
  8.9 83.8 %all-to-all-start = ((bf16[64,64,256]{2,1,0:T(8,128)(2,1)}), bf16[64,64,256]{2,1,0:T(8,128)(2,1)S(1)}, u32[]{:S(2)}, u32[]{:S(2)}) async-start(bf16[64,64,256]{2,1,0:T(8,128)(2,1)} %stack.2), calls=%async_computation | async-start | bytes 4194304 | tf_op jit(solution)/shard_map/all_to_all | solution.py:27
  25.7 107.2 %all-gather.3.cloned.1.call-start = ((), (), s32[]{:S(2)}) async-start(), calls=%async_computation.3 | async-start | bytes 2129920 | tf_op jit(solution)/shard_map/all_gather | solution.py:29
  26.4 232.8 %all-gather.5.cloned.1.call-start = ((), (), s32[]{:S(2)}) async-start(), calls=%async_computation.4 | async-start | bytes 2129920 | tf_op jit(solution)/shard_map/all_gather | solution.py:72
  27.2 67.6 %copy-start.4 = (bf16[64,256]{1,0:T(8,128)(2,1)S(1)}, bf16[64,256]{1,0:T(8,128)(2,1)}, u32[]{:S(2)}) copy-start(bf16[64,256]{1,0:T(8,128)(2,1)} %param.12) | copy-start | bytes 98308
  137.0 27.9 %copy-start.2 = (bf16[64,256]{1,0:T(8,128)(2,1)S(1)}, bf16[64,256]{1,0:T(8,128)(2,1)}, u32[]{:S(2)}) copy-start(bf16[64,256]{1,0:T(8,128)(2,1)} %param.11) | copy-start | bytes 98308
  137.0 40.1 %copy-start.3 = (f32[2048]{0:T(1024)S(1)}, f32[2048]{0:T(1024)}, u32[]{:S(2)}) copy-start(f32[2048]{0:T(1024)} %param.16) | copy-start | bytes 24580
  177.9 242.1 %reduce-scatter.2.cloned.1.call-start = ((), (), s32[]{:S(2)}) async-start(), calls=%async_computation.5 | async-start | bytes 4259840 | tf_op jit(solution)/shard_map/reduce_scatter | solution.py:77
  259.2 2.5 copy-start.1
Sparse Core Ops, SparseCore 0:
  29.8 103.0 all-gather.2
  178.0 81.1 all-gather.4
  267.4 152.5 reduce-scatter.1
